TPU v7x, 32 devices: a whole 2x2x4 slice. The times are simulated.
32 devices in a mesh: groups: 2 (over x), expert: 16 (over z, y, core).
Axes of the slice: x: 2, y: 2, z: 4, core: 2. Of those that a mesh axis runs over, the one named last changes fastest.
Arguments:
- tokens: bfloat16 [2048, 2048], P(('groups', 'expert')), parts along dimension 0, may hold values from -6 to 6
- expert_ids: int32 [2048, 8], P(('groups', 'expert')), parts along dimension 0, may hold values from 0 to 15, as said below
- gate_weights: float32 [2048, 8], P(('groups', 'expert')), parts along dimension 0, may hold values from 0.05 to 0.5
- w_gate: bfloat16 [16, 2048, 768], P('expert'), may hold values from -0.125 to 0.125
- w_up: bfloat16 [16, 2048, 768], P('expert'), may hold values from -0.125 to 0.125
- w_down: bfloat16 [16, 768, 2048], P('expert'), may hold values from -0.21875 to 0.21875
Outputs:
- mixed: bfloat16 [2048, 2048], P(('groups', 'expert')), parts along dimension 0
There are 2 independent parts, one for each index of `groups`. A program takes and returns all parts, laid end to end along the dimension named above; an argument that names none is the same for every part. Nothing has to cross between parts.
Inputs may be any that keep to these rules, and one draw needn't show every extreme that they name: `expert_ids`: each token names 8 different experts. Exactly 2 experts are named exactly 64 times by the tokens of every device; every other expert is named at most 28 times by the tokens of one device, and in every draw some such expert is named exactly 28 times by the tokens of every device.
All inputs are finite; a program needn't handle non-finite values.
Results may differ from a plain program's by a relative error of at most 0.0057.
Values may be sent and summed in bfloat16 or wider, within the bound.
A program may use at most 128 MiB of HBM per device.

v0:
```python
import jax
import jax.numpy as jnp
from jax import lax
from jax.sharding import PartitionSpec as P

row_block = 256


def swiglu_rows(rows_in, weights):
    gate_part = jnp.dot(rows_in, weights[0], preferred_element_type=jnp.float32)
    up_part = jnp.dot(rows_in, weights[1], preferred_element_type=jnp.float32)
    hidden = (jax.nn.silu(gate_part) * up_part).astype(jnp.bfloat16)
    return jnp.dot(hidden, weights[2], preferred_element_type=jnp.float32).astype(jnp.bfloat16)


def run_blocks(source_rows, block_total, weights, results):

    def block_step(block_num, current):
        row_start = block_num * row_block
        rows_in = lax.dynamic_slice_in_dim(source_rows, row_start, row_block, 0)
        return lax.dynamic_update_slice_in_dim(current, swiglu_rows(rows_in, weights), row_start, 0)

    return lax.fori_loop(jnp.zeros((), jnp.int32), block_total, block_step, results)


def route_and_run(tokens, flat_ids, slot_rank, routed, capacity, device_count, own_weights):
    local_tokens, model_width = tokens.shape
    slot_total = flat_ids.shape[0]
    top_count = slot_total // local_tokens
    buffer_rows = device_count * capacity
    padded_rows = (buffer_rows + row_block - 1) // row_block * row_block
    send_slot = jnp.where(routed, flat_ids * capacity + slot_rank, buffer_rows)
    token_of_slot = jnp.arange(slot_total, dtype=jnp.int32) // top_count
    source_row = jnp.zeros((buffer_rows,), jnp.int32).at[send_slot].set(token_of_slot, mode="drop")
    slot_filled = jnp.zeros((buffer_rows,), jnp.int32).at[send_slot].set(1, mode="drop")
    send_counts = jnp.sum(slot_filled.reshape(device_count, capacity), axis=1)
    outgoing = jnp.where(slot_filled[:, None] > 0, tokens[source_row], jnp.zeros((), jnp.bfloat16))
    outgoing = outgoing.reshape(device_count, capacity, model_width)
    count_column = send_counts.astype(jnp.bfloat16).reshape(device_count, 1)
    incoming, arrived = (
        lax.all_to_all(outgoing, "expert", split_axis=0, concat_axis=0, tiled=True),
        lax.all_to_all(count_column, "expert", split_axis=0, concat_axis=0, tiled=True),
    )
    arrived_counts = arrived.reshape(-1).astype(jnp.int32)
    offsets = jnp.cumsum(arrived_counts) - arrived_counts
    live_total = jnp.sum(arrived_counts)
    slot_index = jnp.arange(buffer_rows, dtype=jnp.int32)
    source_of = slot_index // capacity
    within = slot_index % capacity
    is_live = within < arrived_counts[source_of]
    packed_pos = offsets[source_of] + within
    target_pos = jnp.where(is_live, packed_pos, padded_rows)
    compact_source = (
        jnp.full((padded_rows,), buffer_rows, jnp.int32).at[target_pos].set(slot_index, mode="drop")
    )
    flat_incoming = jnp.concatenate(
        [incoming.reshape(buffer_rows, model_width), jnp.zeros((1, model_width), jnp.bfloat16)],
        axis=0,
    )
    compact = flat_incoming[compact_source]
    block_need = (live_total + row_block - 1) // row_block
    results = run_blocks(
        compact, block_need, own_weights, jnp.zeros((padded_rows, model_width), jnp.bfloat16)
    )
    back_slots = results[jnp.where(is_live, packed_pos, 0)]
    back_slots = jnp.where(is_live[:, None], back_slots, jnp.zeros((), jnp.bfloat16))
    back_slots = back_slots.reshape(device_count, capacity, model_width)
    returned_rows = lax.all_to_all(back_slots, "expert", split_axis=0, concat_axis=0, tiled=True)
    picked = returned_rows.reshape(buffer_rows, model_width)[jnp.where(routed, send_slot, 0)]
    return jnp.where(routed[:, None], picked, jnp.zeros((), jnp.bfloat16))


def shards(tokens, expert_ids, gate_weights, w_gate, w_up, w_down):
    device_count = lax.axis_size("expert")
    local_tokens, model_width = tokens.shape
    top_count = expert_ids.shape[1]
    expert_total = device_count * w_gate.shape[0]
    capacity = min(
        local_tokens, 4 * ((local_tokens * top_count + expert_total - 1) // expert_total)
    )
    flat_ids = expert_ids.reshape(-1)
    slot_total = flat_ids.shape[0]
    expert_range = jnp.arange(device_count, dtype=jnp.int32)
    onehot = (flat_ids[:, None] == expert_range[None, :]).astype(jnp.int32)
    slot_rank = jnp.sum(jnp.cumsum(onehot, axis=0) * onehot, axis=1) - 1
    own_weights = (w_gate[0], w_up[0], w_down[0])
    routed = jnp.ones((slot_total,), jnp.bool_)
    slot_values = route_and_run(
        tokens, flat_ids, slot_rank, routed, capacity, device_count, own_weights
    )
    picked = slot_values.reshape(local_tokens, top_count, model_width)
    mixed = jnp.sum(picked.astype(jnp.float32) * gate_weights[:, :, None], axis=1)
    return mixed.astype(jnp.bfloat16)


def solution(mesh):
    placed = (
        P(("groups", "expert"), None),
        P(("groups", "expert"), None),
        P(("groups", "expert"), None),
        P("expert", None, None),
        P("expert", None, None),
        P("expert", None, None),
    )
    return jax.shard_map(
        shards, mesh=mesh, in_specs=placed, out_specs=P(("groups", "expert"), None), check_vma=False
    )
```

profile of v0, /device:TPU:15, one launch (start us, length us, event | category | flops | bytes accessed | tf_op | source)
XLA Modules:
  0.0 305.7 jit_solution(18314291863465316378)
XLA Ops:
  0.0 0.8 copy.30
  1.0 0.7 broadcast_multiply_fusion
  1.7 1.1 reduce-window.19
  3.4 2.4 scatter_custom_fusion
  6.1 0.7 copy.33
  6.8 6.5 %all-to-all-start = ((bf16[16,1,1]{2,1,0:T(2,128)(2,1)}), bf16[16,1,1]{2,1,0:T(2,128)(2,1)S(1)}, u32[]{:S(2)}, u32[]{:S(2)}) async-start(bf16[16,1,1]{2,1,0:T(2,128)(2,1)} %copy.33), calls=%async_computation | async-start | bytes 16384 | tf_op jit(solution)/shard_map/all_to_all | solution.py:42
  13.4 2.4 scatter_custom_fusion.1
  15.9 6.0 %gather_fusion = bf16[1024,2048]{1,0:T(8,128)(2,1)} fusion(bf16[64,2048]{1,0:T(8,128)(2,1)S(1)} %copy-done, s32[1024]{0:T(1024)S(1)} %fusion.20), kind=kCustom, calls=%fused_computation | custom fusion | bytes 8392704 | tf_op jit(solution)/shard_map/gather | solution.py:37
  21.9 4.5 %broadcast_select_fusion = bf16[16,64,2048]{2,1,0:T(8,128)(2,1)} fusion(bf16[16,64,2048]{2,1,0:T(8,128)(2,1)} %bitcast.78, pred[16,64]{1,0:T(8,128)(4,1)S(1)} %broadcast_in_dim.61), kind=kLoop, calls=%fused_computation.20 | loop fusion | flops 2097152 | bytes 8389632 | tf_op jit(solution)/shard_map/jit(_where)/select_n | solution.py:37
  26.4 6.0 %all-to-all-start.1 = ((bf16[16,64,2048]{2,1,0:T(8,128)(2,1)}), bf16[16,64,2048]{2,1,0:T(8,128)(2,1)}, u32[]{:S(2)}, u32[]{:S(2)}) async-start(bf16[16,64,2048]{2,1,0:T(8,128)(2,1)} %broadcast_select_fusion), calls=%async_computation.1 | async-start | bytes 8388608 | tf_op jit(solution)/shard_map/all_to_all | solution.py:41
  32.7 0.9 convert_reduce_fusion.1
  35.1 4.2 %compare_select_fusion.6 = s32[1024,1]{0,1:T(1,128)S(1)} fusion(s32[]{:T(128)} %bitcast.13, s32[]{:T(128)} %bitcast.14, s32[]{:T(128)} %bitcast.15, s32[]{:T(128)} %bitcast.16, s32[]{:T(128)} %bitcast.17, s32[]{:T(128)} %bitcast.19, s32[]{:T(128)} %bitcast.18), kind=kLoop, calls=%fused_computation.48 | loop fusion | flops 23552 | bytes 4124 | tf_op jit(solution)/shard_map/gather | solution.py:50
  39.3 5.7 %select_select_fusion.1 = s32[1024]{0:T(1024)S(1)} fusion(pred[1024]{0:T(1024)(128)(4,1)S(1)} %compare_reduce_fusion, pred[1024]{0:T(1024)(128)(4,1)S(1)} %compare_reduce_fusion.1, pred[1024]{0:T(1024)(128)(4,1)S(1)} %compare_reduce_fusion.2, pred[1024]{0:T(1024)(128)(4,1)S(1)} %compare_reduce_fusion.3, pred[1024]{0:T(1024)(128)(4,1)S(1)} %compare_reduce_fusion.4, ...), kind=kLoop, calls=%fused_computation.72 | loop fusion | flops 9216 | bytes 17444 | tf_op jit(solution)/shard_map/gather | solution.py:50
  45.1 0.7 fusion.34
  45.8 4.5 %compare_select_fusion.7 = s32[1024,1]{0,1:T(1,128)S(1)} fusion(s32[]{:T(128)} %bitcast.34, s32[]{:T(128)} %bitcast.35, s32[]{:T(128)} %bitcast.36, s32[]{:T(128)} %bitcast.37, s32[]{:T(128)} %bitcast.38, s32[]{:T(128)} %bitcast.40, s32[]{:T(128)} %bitcast.39), kind=kLoop, calls=%fused_computation.49 | loop fusion | flops 23552 | bytes 4124 | tf_op jit(solution)/shard_map/gather | solution.py:51
  50.3 5.4 %select_select_fusion = s32[1024]{0:T(1024)S(1)} fusion(pred[1024]{0:T(1024)(128)(4,1)S(1)} %compare_reduce_fusion, pred[1024]{0:T(1024)(128)(4,1)S(1)} %compare_reduce_fusion.1, pred[1024]{0:T(1024)(128)(4,1)S(1)} %compare_reduce_fusion.2, pred[1024]{0:T(1024)(128)(4,1)S(1)} %compare_reduce_fusion.3, pred[1024]{0:T(1024)(128)(4,1)S(1)} %compare_reduce_fusion.4, ...), kind=kLoop, calls=%fused_computation.71 | loop fusion | flops 9216 | bytes 17444 | tf_op jit(solution)/shard_map/gather | solution.py:51
  55.8 4.3 %scatter_custom_fusion.2 = s32[1024]{0:T(1024)S(1)} fusion(s32[1024]{0:T(1024)S(1)} %bitcast.89, s32[1024]{0:T(1024)S(1)} %iota.46, s32[]{:T(128)} %constant.94.clone.1), kind=kCustom, calls=%fused_computation.80 | custom fusion | bytes 4100 | tf_op jit(solution)/shard_map/scatter | solution.py:54
  60.2 64.7 %all-to-all-done.1 = bf16[16,64,2048]{2,1,0:T(8,128)(2,1)} async-done(((bf16[16,64,2048]{2,1,0:T(8,128)(2,1)}), bf16[16,64,2048]{2,1,0:T(8,128)(2,1)}, u32[]{:S(2)}, u32[]{:S(2)}) %all-to-all-start.1) | async-done | bytes 4194336 | tf_op jit(solution)/shard_map/all_to_all | solution.py:41
  124.8 4.7 %concatenate.3 = bf16[1025,2048]{1,0:T(8,128)(2,1)} pad(bf16[1024,2048]{1,0:T(8,128)(2,1)} %bitcast.22, bf16[]{:T(256)} %constant.98.clone.1), padding=0_1x0_0 | pad | bytes 8392706 | tf_op jit(solution)/shard_map/concatenate | solution.py:56
  129.6 11.6 %gather_fusion.1 = bf16[1024,2048]{1,0:T(8,128)(2,1)} fusion(bf16[1025,2048]{1,0:T(8,128)(2,1)} %concatenate.3, s32[1024]{0:T(1024)S(1)} %fusion.21), kind=kCustom, calls=%fused_computation.1 | custom fusion | bytes 8392704 | tf_op jit(solution)/shard_map/gather | solution.py:60
  141.1 2.5 broadcast_in_dim.60
  144.0 19.3 %while.10 = (s32[]{:T(128)}, bf16[1024,2048]{1,0:T(8,128)(2,1)}, s32[]{:T(128)}, bf16[1024,2048]{1,0:T(8,128)(2,1)}, bf16[2048,768]{1,0:T(8,128)(2,1)S(1)}, /*in...) while((s32[]{:T(128)}, bf16[1024,2048]{1,0:T(8,128)(2,1)}, ...), condition=%wide.region_10.11_spmd, body=%wide.region_9.10_spmd.sunk | while | flops 2417623040 | bytes 14156959 | solution.py:23
  144.0 3.1 %fusion.50 = f32[256,768]{1,0:T(8,128)} fusion(bf16[2048,768]{1,0:T(8,128)(2,1)S(1)} %get-tuple-element.164, bf16[1024,2048]{1,0:T(8,128)(2,1)} %get-tuple-element.163, s32[]{:T(128)S(6)} %select_n.234), kind=kOutput, calls=%fused_computation.12.clone.1 | convolution fusion | flops 805306368 | bytes 4980740 | tf_op jit(solution)/shard_map/while/body/dot_general | solution.py:10
  147.2 6.6 %fusion.51 = bf16[1024,2048]{1,0:T(8,128)(2,1)} fusion(bf16[1024,2048]{1,0:T(8,128)(2,1)} %get-tuple-element.150, s32[]{:T(128)S(6)} %select_n.234, bf16[768,2048]{1,0:T(8,128)(2,1)} %get-tuple-element.166, bf16[2048,768]{1,0:T(8,128)(2,1)} %get-tuple-element.165, bf16[1024,2048]{1,0:T(8,128)(2,1)} %get-tuple-element.163, f32[256,768]{1,0:T(8,128)} %fusion.50), kind=kOutput, calls=%fused_computation.8.clone.1 | convolution fusion | flops 1612316672 | bytes 9176064 | tf_op jit(solution)/shard_map/while/body/dot_general | solution.py:13
  153.7 3.1 %fusion.50 = f32[256,768]{1,0:T(8,128)} fusion(bf16[2048,768]{1,0:T(8,128)(2,1)S(1)} %get-tuple-element.164, bf16[1024,2048]{1,0:T(8,128)(2,1)} %get-tuple-element.163, s32[]{:T(128)S(6)} %select_n.234), kind=kOutput, calls=%fused_computation.12.clone.1 | convolution fusion | flops 805306368 | bytes 4980740 | tf_op jit(solution)/shard_map/while/body/dot_general | solution.py:10
  156.8 6.5 %fusion.51 = bf16[1024,2048]{1,0:T(8,128)(2,1)} fusion(bf16[1024,2048]{1,0:T(8,128)(2,1)} %get-tuple-element.150, s32[]{:T(128)S(6)} %select_n.234, bf16[768,2048]{1,0:T(8,128)(2,1)} %get-tuple-element.166, bf16[2048,768]{1,0:T(8,128)(2,1)} %get-tuple-element.165, bf16[1024,2048]{1,0:T(8,128)(2,1)} %get-tuple-element.163, f32[256,768]{1,0:T(8,128)} %fusion.50), kind=kOutput, calls=%fused_computation.8.clone.1 | convolution fusion | flops 1612316672 | bytes 9176064 | tf_op jit(solution)/shard_map/while/body/dot_general | solution.py:13
  163.3 11.6 %gather_fusion.2 = bf16[1024,2048]{1,0:T(8,128)(2,1)} fusion(bf16[1024,2048]{1,0:T(8,128)(2,1)} %get-tuple-element.43, s32[1024]{0:T(1024)S(1)} %broadcast_clamp_fusion), kind=kCustom, calls=%fused_computation.2 | custom fusion | bytes 8392704 | tf_op jit(solution)/shard_map/gather | solution.py:65
  174.9 4.5 %broadcast_select_fusion.1 = bf16[16,64,2048]{2,1,0:T(8,128)(2,1)} fusion(bf16[16,64,2048]{2,1,0:T(8,128)(2,1)} %bitcast.77, pred[16,64]{1,0:T(8,128)(4,1)S(1)} %fusion.16), kind=kLoop, calls=%fused_computation.21 | loop fusion | flops 2097152 | bytes 8389632 | tf_op jit(solution)/shard_map/jit(_where)/select_n | solution.py:66
  179.4 24.2 %all-to-all-start.2 = ((bf16[16,64,2048]{2,1,0:T(8,128)(2,1)}), bf16[16,64,2048]{2,1,0:T(8,128)(2,1)}, u32[]{:S(2)}, u32[]{:S(2)}) async-start(bf16[16,64,2048]{2,1,0:T(8,128)(2,1)} %broadcast_select_fusion.1), calls=%async_computation.2 | async-start | bytes 8388608 | tf_op jit(solution)/shard_map/all_to_all | solution.py:68
  203.7 92.4 %all-to-all-done.2 = bf16[16,64,2048]{2,1,0:T(8,128)(2,1)} async-done(((bf16[16,64,2048]{2,1,0:T(8,128)(2,1)}), bf16[16,64,2048]{2,1,0:T(8,128)(2,1)}, u32[]{:S(2)}, u32[]{:S(2)}) %all-to-all-start.2) | async-done | bytes 4194336 | tf_op jit(solution)/shard_map/all_to_all | solution.py:68
  296.0 7.1 %gather_fusion.3 = bf16[512,2048]{1,0:T(8,128)(2,1)S(1)} fusion(bf16[1024,2048]{1,0:T(8,128)(2,1)} %bitcast.49, s32[1024]{0:T(1024)S(1)} %pad_clamp_fusion), kind=kCustom, calls=%fused_computation.3 | custom fusion | bytes 4196352 | tf_op jit(solution)/shard_map/gather | solution.py:69
  303.2 2.5 fusion.12
  (48 shorter events, 2.8 us)
Async XLA Ops:
  0.0 15.9 %copy-start = (bf16[64,2048]{1,0:T(8,128)(2,1)S(1)}, bf16[64,2048]{1,0:T(8,128)(2,1)}, u32[]{:S(2)}) copy-start(bf16[64,2048]{1,0:T(8,128)(2,1)} %param.8) | copy-start | bytes 786436
  6.8 19.6 %all-to-all-start = ((bf16[16,1,1]{2,1,0:T(2,128)(2,1)}), bf16[16,1,1]{2,1,0:T(2,128)(2,1)S(1)}, u32[]{:S(2)}, u32[]{:S(2)}) async-start(bf16[16,1,1]{2,1,0:T(2,128)(2,1)} %copy.33), calls=%async_computation | async-start | bytes 16384 | tf_op jit(solution)/shard_map/all_to_all | solution.py:42
  26.4 98.5 %all-to-all-start.1 = ((bf16[16,64,2048]{2,1,0:T(8,128)(2,1)}), bf16[16,64,2048]{2,1,0:T(8,128)(2,1)}, u32[]{:S(2)}, u32[]{:S(2)}) async-start(bf16[16,64,2048]{2,1,0:T(8,128)(2,1)} %broadcast_select_fusion), calls=%async_computation.1 | async-start | bytes 8388608 | tf_op jit(solution)/shard_map/all_to_all | solution.py:41
  141.1 2.9 copy-start.2
  179.4 24.2 %copy-start.1 = (f32[64,8]{0,1:T(8,128)S(1)}, f32[64,8]{0,1:T(8,128)}, u32[]{:S(2)}) copy-start(f32[64,8]{0,1:T(8,128)} %param.10) | copy-start | bytes 6148
  179.4 116.6 %all-to-all-start.2 = ((bf16[16,64,2048]{2,1,0:T(8,128)(2,1)}), bf16[16,64,2048]{2,1,0:T(8,128)(2,1)}, u32[]{:S(2)}, u32[]{:S(2)}) async-start(bf16[16,64,2048]{2,1,0:T(8,128)(2,1)} %broadcast_select_fusion.1), calls=%async_computation.2 | async-start | bytes 8388608 | tf_op jit(solution)/shard_map/all_to_all | solution.py:68
where the time goes:
time: 307 us; the launch traced here: 306 us
  waiting for transfers between devices  157 us (51%)
  local copies, waits for them, and re-layouts  56.8 us (19%)
  starting transfers between devices  36.7 us (12%)
  other arithmetic  35 us (11%)
  matrix products  19.3 us (6%)
    all_to_all x1, waiting for transfers between devices, route_and_run(): lax.all_to_all(back_slots, 'expert', split_axis=0, concat_axis=0, tiled=T...  92.4 us
    all_to_all x1, waiting for transfers between devices, route_and_run(): lax.all_to_all(outgoing, 'expert', split_axis=0, concat_axis=0, tiled=True)  64.7 us
    all_to_all x1, starting transfers between devices, route_and_run(): lax.all_to_all(back_slots, 'expert', split_axis=0, concat_axis=0, tiled=T...  24.2 us
    dot_general x2, matrix products, swiglu_rows(): jnp.dot(hidden, weights[2], preferred_element_type=jnp.float32)  13.1 us
    gather x1, local copies, waits for them, and re-layouts, route_and_run(): compact = flat_incoming[compact_source]  11.6 us
    gather x1, local copies, waits for them, and re-layouts, route_and_run(): back_slots = results[jnp.where(is_live, packed_pos, 0)]  11.6 us
    gather x11, other arithmetic, route_and_run(): is_live = within < arrived_counts[source_of]  10.2 us
    gather x2, other arithmetic, route_and_run(): packed_pos = offsets[source_of] + within  9.94 us
  transfers between devices with their start and end apart: 3, of which 2 were waited for; matrix products, arithmetic and copies ran while one was open for 13% of the time, Pallas kernels for 0%

commit v1 on v0

--- a/solution.py
+++ b/solution.py
@@ -4,6 +4,29 @@
 from jax.sharding import PartitionSpec as P
 
 row_block = 256
+
+
+def in_blocks(value, dim, length):
+    shape = value.shape
+    parts = value.reshape(*shape[:dim], length, shape[dim] // length, *shape[dim + 1 :])
+    return jnp.moveaxis(parts, dim, 0)
+
+
+def laid_out(blocks, dim):
+    shape = list(blocks.shape[1:])
+    shape[dim] *= blocks.shape[0]
+    return jnp.moveaxis(blocks, 0, dim).reshape(shape)
+
+
+def pairwise_exchange(x, axis, split_dim, concat_dim):
+    devices, place = (lax.axis_size(axis), lax.axis_index(axis))
+    blocks = in_blocks(x, split_dim, devices)
+    done = [blocks[place]]
+    for step in range(1, devices):
+        sent = blocks[place ^ step]
+        done.append(lax.ppermute(sent, axis, [(i, i ^ step) for i in range(devices)]))
+    blocks = jnp.stack(done)[place ^ jnp.arange(devices)]
+    return laid_out(blocks, concat_dim)
 
 
 def swiglu_rows(rows_in, weights):
@@ -65,7 +88,7 @@
     back_slots = results[jnp.where(is_live, packed_pos, 0)]
     back_slots = jnp.where(is_live[:, None], back_slots, jnp.zeros((), jnp.bfloat16))
     back_slots = back_slots.reshape(device_count, capacity, model_width)
-    returned_rows = lax.all_to_all(back_slots, "expert", split_axis=0, concat_axis=0, tiled=True)
+    returned_rows = pairwise_exchange(back_slots, "expert", 0, 0)
     picked = returned_rows.reshape(buffer_rows, model_width)[jnp.where(routed, send_slot, 0)]
     return jnp.where(routed[:, None], picked, jnp.zeros((), jnp.bfloat16))
 

time: 307 us -> 319 us (1.039)
  waiting for transfers between devices: 157 us -> 134 us
  local copies, waits for them, and re-layouts: 56.8 us -> 74.9 us
  starting transfers between devices: 36.7 us -> 53.7 us
    all_to_all x1 -> x0, waiting for transfers between devices: 92.4 us -> none  [route_and_run(): lax.all_to_all(back_slots, 'expert', split_axis=0, concat_axis=0, tiled=T...]
    ppermute x0 -> x15, waiting for transfers between devices: none -> 69.4 us  [pairwise_exchange(): lax.ppermute(sent, axis, [(i, i ^ step) for i in range(devices)])]
    ppermute x0 -> x15, starting transfers between devices: none -> 41.1 us  [pairwise_exchange(): lax.ppermute(sent, axis, [(i, i ^ step) for i in range(devices)])]
    all_to_all x1 -> x0, starting transfers between devices: 24.2 us -> none  [route_and_run(): lax.all_to_all(back_slots, 'expert', split_axis=0, concat_axis=0, tiled=T...]
    unnamed x8 -> x22, local copies, waits for them, and re-layouts: 1.31 us -> 12.5 us
    gather x0 -> x1, local copies, waits for them, and re-layouts: none -> 4.97 us  [pairwise_exchange(): blocks = jnp.stack(done)[place ^ jnp.arange(devices)]]
    gather x2 -> x1, other arithmetic: 9.94 us -> 5.55 us  [route_and_run(): packed_pos = offsets[source_of] + within]
    gather x11 -> x7, other arithmetic: 10.2 us -> 14.4 us  [route_and_run(): is_live = within < arrived_counts[source_of]]
  transfers between devices with their start and end apart: 3 -> 17, of which waited for: 2 -> 9; matrix products, arithmetic and copies ran while one was open for 13% -> 16% of each run, Pallas kernels for 0% -> 0%
where the time goes in v1:
time: 319 us; the launch traced here: 316 us
  waiting for transfers between devices  134 us (42%)
  local copies, waits for them, and re-layouts  74.9 us (23%)
  starting transfers between devices  53.7 us (17%)
  other arithmetic  32.8 us (10%)
  matrix products  19.4 us (6%)
    ppermute x15, waiting for transfers between devices, pairwise_exchange(): lax.ppermute(sent, axis, [(i, i ^ step) for i in range(devices)])  69.4 us
    all_to_all x1, waiting for transfers between devices, route_and_run(): lax.all_to_all(outgoing, 'expert', split_axis=0, concat_axis=0, tiled=True)  64.9 us
    ppermute x15, starting transfers between devices, pairwise_exchange(): lax.ppermute(sent, axis, [(i, i ^ step) for i in range(devices)])  41.1 us
    gather x7, other arithmetic, route_and_run(): is_live = within < arrived_counts[source_of]  14.4 us
    dot_general x2, matrix products, swiglu_rows(): jnp.dot(hidden, weights[2], preferred_element_type=jnp.float32)  13.1 us
    unnamed x22, local copies, waits for them, and re-layouts  12.5 us
    gather x1, local copies, waits for them, and re-layouts, route_and_run(): compact = flat_incoming[compact_source]  11.6 us
    gather x1, local copies, waits for them, and re-layouts, route_and_run(): back_slots = results[jnp.where(is_live, packed_pos, 0)]  11.6 us
  transfers between devices with their start and end apart: 17, of which 9 were waited for; matrix products, arithmetic and copies ran while one was open for 16% of the time, Pallas kernels for 0%

profile of v1, /device:TPU:15, one launch (start us, length us, event | category | flops | bytes accessed | tf_op | source)
XLA Modules:
  0.0 315.9 jit_solution(6217946692218486371)
XLA Ops:
  6.8 6.5 %all-to-all-start = ((bf16[16,1,1]{2,1,0:T(2,128)(2,1)}), bf16[16,1,1]{2,1,0:T(2,128)(2,1)S(1)}, u32[]{:S(2)}, u32[]{:S(2)}) async-start(bf16[16,1,1]{2,1,0:T(2,128)(2,1)} %copy.33), calls=%async_computation | async-start | bytes 16384 | tf_op jit(solution)/shard_map/all_to_all | solution.py:65
  15.9 6.0 %gather_fusion = bf16[1024,2048]{1,0:T(8,128)(2,1)} fusion(bf16[64,2048]{1,0:T(8,128)(2,1)S(1)} %copy-done, s32[1024]{0:T(1024)S(1)} %get-tuple-element.120), kind=kCustom, calls=%fused_computation | custom fusion | bytes 8392704 | tf_op jit(solution)/shard_map/gather | solution.py:60
  21.9 4.5 %broadcast_select_fusion = bf16[16,64,2048]{2,1,0:T(8,128)(2,1)} fusion(bf16[16,64,2048]{2,1,0:T(8,128)(2,1)} %bitcast.142, pred[16,64]{1,0:T(8,128)(4,1)S(1)} %broadcast_in_dim.64), kind=kLoop, calls=%fused_computation.21 | loop fusion | flops 2097152 | bytes 8389632 | tf_op jit(solution)/shard_map/jit(_where)/select_n | solution.py:60
  26.4 6.0 %all-to-all-start.1 = ((bf16[16,64,2048]{2,1,0:T(8,128)(2,1)}), bf16[16,64,2048]{2,1,0:T(8,128)(2,1)}, u32[]{:S(2)}, u32[]{:S(2)}) async-start(bf16[16,64,2048]{2,1,0:T(8,128)(2,1)} %broadcast_select_fusion), calls=%async_computation.1 | async-start | bytes 8388608 | tf_op jit(solution)/shard_map/all_to_all | solution.py:64
  35.6 8.7 %compare_select_fusion.6 = (s32[1024,1]{0,1:T(1,128)S(1)}, s32[1024,1]{0,1:T(1,128)S(1)}) fusion(s32[]{:T(128)} %bitcast.13, s32[]{:T(128)} %bitcast.14, s32[]{:T(128)} %bitcast.15, s32[]{:T(128)} %bitcast.16, s32[]{:T(128)} %bitcast.17, s32[]{:T(128)} %bitcast.19, s32[]{:T(128)} %bitcast.18, s32[]{:T(128)} %bitcast.40, s32[]{:T(128)} %bitcast.39, ...), kind=kLoop, calls=%fused_computation.80 | loop fusion | flops 29696 | bytes 8248 | tf_op jit(solution)/shard_map/gather | solution.py:73
  44.3 5.6 %select_select_fusion.1 = s32[1024]{0:T(1024)S(1)} fusion(pred[1024]{0:T(1024)(128)(4,1)S(1)} %get-tuple-element.110, pred[1024]{0:T(1024)(128)(4,1)S(1)} %get-tuple-element.111, pred[1024]{0:T(1024)(128)(4,1)S(1)} %get-tuple-element.112, pred[1024]{0:T(1024)(128)(4,1)S(1)} %get-tuple-element.113, pred[1024]{0:T(1024)(128)(4,1)S(1)} %get-tuple-element.114, ...), kind=kLoop, calls=%fused_computation.105 | loop fusion | flops 9216 | bytes 17444 | tf_op jit(solution)/shard_map/gather | solution.py:73
  50.0 5.5 %select_select_fusion = s32[1024]{0:T(1024)S(1)} fusion(pred[1024]{0:T(1024)(128)(4,1)S(1)} %get-tuple-element.110, pred[1024]{0:T(1024)(128)(4,1)S(1)} %get-tuple-element.111, pred[1024]{0:T(1024)(128)(4,1)S(1)} %get-tuple-element.112, pred[1024]{0:T(1024)(128)(4,1)S(1)} %get-tuple-element.113, pred[1024]{0:T(1024)(128)(4,1)S(1)} %get-tuple-element.114, ...), kind=kLoop, calls=%fused_computation.104 | loop fusion | flops 9216 | bytes 17444 | tf_op jit(solution)/shard_map/gather | solution.py:74
  55.5 4.3 %scatter_custom_fusion.2 = s32[1024]{0:T(1024)S(1)} fusion(s32[1024]{0:T(1024)S(1)} %bitcast.154, s32[1024]{0:T(1024)S(1)} %iota.50, s32[]{:T(128)} %constant.113.clone.1), kind=kCustom, calls=%fused_computation.114 | custom fusion | bytes 4100 | tf_op jit(solution)/shard_map/scatter | solution.py:77
  59.9 64.9 %all-to-all-done.1 = bf16[16,64,2048]{2,1,0:T(8,128)(2,1)} async-done(((bf16[16,64,2048]{2,1,0:T(8,128)(2,1)}), bf16[16,64,2048]{2,1,0:T(8,128)(2,1)}, u32[]{:S(2)}, u32[]{:S(2)}) %all-to-all-start.1) | async-done | bytes 4194336 | tf_op jit(solution)/shard_map/all_to_all | solution.py:64
  124.8 4.7 %concatenate.3 = bf16[1025,2048]{1,0:T(8,128)(2,1)} pad(bf16[1024,2048]{1,0:T(8,128)(2,1)} %bitcast.22, bf16[]{:T(256)} %constant.117.clone.1), padding=0_1x0_0 | pad | bytes 8392706 | tf_op jit(solution)/shard_map/concatenate | solution.py:79
  129.6 11.6 %gather_fusion.1 = bf16[1024,2048]{1,0:T(8,128)(2,1)} fusion(bf16[1025,2048]{1,0:T(8,128)(2,1)} %concatenate.3, s32[1024]{0:T(1024)S(1)} %fusion.21), kind=kCustom, calls=%fused_computation.1 | custom fusion | bytes 8392704 | tf_op jit(solution)/shard_map/gather | solution.py:83
  144.0 19.4 %while.10 = (s32[]{:T(128)}, bf16[1024,2048]{1,0:T(8,128)(2,1)}, s32[]{:T(128)}, bf16[1024,2048]{1,0:T(8,128)(2,1)}, bf16[2048,768]{1,0:T(8,128)(2,1)S(1)}, /*in...) while((s32[]{:T(128)}, bf16[1024,2048]{1,0:T(8,128)(2,1)}, ...), condition=%wide.region_10.11_spmd, body=%wide.region_9.10_spmd.sunk | while | flops 2417623040 | bytes 14156959 | solution.py:46
  144.0 3.1 fusion.51
  147.2 6.5 %fusion.52 = bf16[1024,2048]{1,0:T(8,128)(2,1)} fusion(bf16[1024,2048]{1,0:T(8,128)(2,1)} %get-tuple-element.178, s32[]{:T(128)S(6)} %select_n.318, bf16[768,2048]{1,0:T(8,128)(2,1)} %get-tuple-element.194, bf16[2048,768]{1,0:T(8,128)(2,1)} %get-tuple-element.193, bf16[1024,2048]{1,0:T(8,128)(2,1)} %get-tuple-element.191, f32[256,768]{1,0:T(8,128)} %fusion.51), kind=kOutput, calls=%fused_computation.9.clone.1 | convolution fusion | flops 1612316672 | bytes 9176064 | tf_op jit(solution)/shard_map/while/body/dot_general | solution.py:36
  153.7 3.2 fusion.51
  156.8 6.6 %fusion.52 = bf16[1024,2048]{1,0:T(8,128)(2,1)} fusion(bf16[1024,2048]{1,0:T(8,128)(2,1)} %get-tuple-element.178, s32[]{:T(128)S(6)} %select_n.318, bf16[768,2048]{1,0:T(8,128)(2,1)} %get-tuple-element.194, bf16[2048,768]{1,0:T(8,128)(2,1)} %get-tuple-element.193, bf16[1024,2048]{1,0:T(8,128)(2,1)} %get-tuple-element.191, f32[256,768]{1,0:T(8,128)} %fusion.51), kind=kOutput, calls=%fused_computation.9.clone.1 | convolution fusion | flops 1612316672 | bytes 9176064 | tf_op jit(solution)/shard_map/while/body/dot_general | solution.py:36
  163.4 11.6 %gather_fusion.2 = bf16[1024,2048]{1,0:T(8,128)(2,1)} fusion(bf16[1024,2048]{1,0:T(8,128)(2,1)} %get-tuple-element.43, s32[1024]{0:T(1024)S(1)} %broadcast_clamp_fusion), kind=kCustom, calls=%fused_computation.2 | custom fusion | bytes 8392704 | tf_op jit(solution)/shard_map/gather | solution.py:88
  181.1 2.8 collective-permute-start.3
  184.3 2.8 collective-permute-start.5
  188.8 4.1 %collective-permute-start.6 = (bf16[1,64,2048]{2,1,0:T(8,128)(2,1)S(1)}, bf16[1,64,2048]{2,1,0:T(8,128)(2,1)S(1)}, u32[]{:S(2)}, u32[]{:S(2)}) collective-permute-start(bf16[1,64,2048]{2,1,0:T(8,128)(2,1)S(1)} %get-tuple-element.68), channel_id=1, source_target_pairs={{0,7},{1,6},{2,5},{3,4},{4,3},{5,2},{6,1},{7,0},{8,15},{9,14},{10,... | collective-permute-start | bytes 786440 | tf_op jit(solution)/shard_map/ppermute | solution.py:27
  193.6 20.1 %collective-permute-start.7 = (bf16[1,64,2048]{2,1,0:T(8,128)(2,1)S(1)}, bf16[1,64,2048]{2,1,0:T(8,128)(2,1)S(1)}, u32[]{:S(2)}, u32[]{:S(2)}) collective-permute-start(bf16[1,64,2048]{2,1,0:T(8,128)(2,1)S(1)} %get-tuple-element.67), channel_id=1, source_target_pairs={{0,8},{1,9},{2,10},{3,11},{4,12},{5,13},{6,14},{7,15},{8,0},{9,1},... | collective-permute-start | bytes 786440 | tf_op jit(solution)/shard_map/ppermute | solution.py:27
  218.3 4.3 %collective-permute-start.10 = (bf16[1,64,2048]{2,1,0:T(8,128)(2,1)S(1)}, bf16[1,64,2048]{2,1,0:T(8,128)(2,1)S(1)}, u32[]{:S(2)}, u32[]{:S(2)}) collective-permute-start(bf16[1,64,2048]{2,1,0:T(8,128)(2,1)S(1)} %get-tuple-element.64), channel_id=1, source_target_pairs={{0,11},{1,10},{2,9},{3,8},{4,15},{5,14},{6,13},{7,12},{8,3},{9,2},... | collective-permute-start | bytes 786440 | tf_op jit(solution)/shard_map/ppermute | solution.py:27
  226.1 18.2 %collective-permute-done.7 = bf16[1,64,2048]{2,1,0:T(8,128)(2,1)S(1)} collective-permute-done((bf16[1,64,2048]{2,1,0:T(8,128)(2,1)S(1)}, bf16[1,64,2048]{2,1,0:T(8,128)(2,1)S(1)}, u32[]{:S(2)}, u32[]{:S(2)}) %collective-permute-start.7) | collective-permute-done | bytes 262176 | tf_op jit(solution)/shard_map/ppermute | solution.py:27
  245.1 10.3 %collective-permute-done.8 = bf16[1,64,2048]{2,1,0:T(8,128)(2,1)S(1)} collective-permute-done((bf16[1,64,2048]{2,1,0:T(8,128)(2,1)S(1)}, bf16[1,64,2048]{2,1,0:T(8,128)(2,1)S(1)}, u32[]{:S(2)}, u32[]{:S(2)}) %collective-permute-start.8) | collective-permute-done | bytes 262176 | tf_op jit(solution)/shard_map/ppermute | solution.py:27
  256.1 5.0 %collective-permute-done.9 = bf16[1,64,2048]{2,1,0:T(8,128)(2,1)S(1)} collective-permute-done((bf16[1,64,2048]{2,1,0:T(8,128)(2,1)S(1)}, bf16[1,64,2048]{2,1,0:T(8,128)(2,1)S(1)}, u32[]{:S(2)}, u32[]{:S(2)}) %collective-permute-start.9) | collective-permute-done | bytes 262176 | tf_op jit(solution)/shard_map/ppermute | solution.py:27
  261.9 16.1 %collective-permute-done.10 = bf16[1,64,2048]{2,1,0:T(8,128)(2,1)S(1)} collective-permute-done((bf16[1,64,2048]{2,1,0:T(8,128)(2,1)S(1)}, bf16[1,64,2048]{2,1,0:T(8,128)(2,1)S(1)}, u32[]{:S(2)}, u32[]{:S(2)}) %collective-permute-start.10) | collective-permute-done | bytes 262176 | tf_op jit(solution)/shard_map/ppermute | solution.py:27
  278.8 4.9 %collective-permute-done.11 = bf16[1,64,2048]{2,1,0:T(8,128)(2,1)S(1)} collective-permute-done((bf16[1,64,2048]{2,1,0:T(8,128)(2,1)S(1)}, bf16[1,64,2048]{2,1,0:T(8,128)(2,1)S(1)}, u32[]{:S(2)}, u32[]{:S(2)}) %collective-permute-start.11) | collective-permute-done | bytes 262176 | tf_op jit(solution)/shard_map/ppermute | solution.py:27
  284.4 4.9 %collective-permute-done.12 = bf16[1,64,2048]{2,1,0:T(8,128)(2,1)S(1)} collective-permute-done((bf16[1,64,2048]{2,1,0:T(8,128)(2,1)S(1)}, bf16[1,64,2048]{2,1,0:T(8,128)(2,1)S(1)}, u32[]{:S(2)}, u32[]{:S(2)}) %collective-permute-start.12) | collective-permute-done | bytes 262176 | tf_op jit(solution)/shard_map/ppermute | solution.py:27
  290.0 5.9 %collective-permute-done.13 = bf16[1,64,2048]{2,1,0:T(8,128)(2,1)S(1)} collective-permute-done((bf16[1,64,2048]{2,1,0:T(8,128)(2,1)S(1)}, bf16[1,64,2048]{2,1,0:T(8,128)(2,1)S(1)}, u32[]{:S(2)}, u32[]{:S(2)}) %collective-permute-start.13) | collective-permute-done | bytes 262176 | tf_op jit(solution)/shard_map/ppermute | solution.py:27
  296.6 3.9 %collective-permute-done.14 = bf16[1,64,2048]{2,1,0:T(8,128)(2,1)S(1)} collective-permute-done((bf16[1,64,2048]{2,1,0:T(8,128)(2,1)S(1)}, bf16[1,64,2048]{2,1,0:T(8,128)(2,1)S(1)}, u32[]{:S(2)}, u32[]{:S(2)}) %collective-permute-start.14) | collective-permute-done | bytes 262176 | tf_op jit(solution)/shard_map/ppermute | solution.py:27
  301.3 5.0 %gather_fusion.3 = bf16[16,64,2048]{2,1,0:T(8,128)(2,1)} fusion(bf16[16,64,2048]{2,1,0:T(8,128)(2,1)} %bitcast.143, s32[1024]{0:T(1024)S(1)} %pad_clamp_fusion.1), kind=kCustom, calls=%fused_computation.3 | custom fusion | bytes 8388672 | tf_op jit(solution)/shard_map/gather | solution.py:28
  306.2 7.1 %gather_fusion.4 = bf16[512,2048]{1,0:T(8,128)(2,1)S(1)} fusion(bf16[1024,2048]{1,0:T(8,128)(2,1)} %bitcast.140, s32[1024]{0:T(1024)S(1)} %get-tuple-element.121), kind=kCustom, calls=%fused_computation.4 | custom fusion | bytes 4196352 | tf_op jit(solution)/shard_map/gather | solution.py:92
  (89 shorter events, 40.2 us)
Async XLA Ops:
  0.0 15.9 %copy-start = (bf16[64,2048]{1,0:T(8,128)(2,1)S(1)}, bf16[64,2048]{1,0:T(8,128)(2,1)}, u32[]{:S(2)}) copy-start(bf16[64,2048]{1,0:T(8,128)(2,1)} %param.8) | copy-start | bytes 786436
  6.8 19.6 %all-to-all-start = ((bf16[16,1,1]{2,1,0:T(2,128)(2,1)}), bf16[16,1,1]{2,1,0:T(2,128)(2,1)S(1)}, u32[]{:S(2)}, u32[]{:S(2)}) async-start(bf16[16,1,1]{2,1,0:T(2,128)(2,1)} %copy.33), calls=%async_computation | async-start | bytes 16384 | tf_op jit(solution)/shard_map/all_to_all | solution.py:65
  26.4 98.5 %all-to-all-start.1 = ((bf16[16,64,2048]{2,1,0:T(8,128)(2,1)}), bf16[16,64,2048]{2,1,0:T(8,128)(2,1)}, u32[]{:S(2)}, u32[]{:S(2)}) async-start(bf16[16,64,2048]{2,1,0:T(8,128)(2,1)} %broadcast_select_fusion), calls=%async_computation.1 | async-start | bytes 8388608 | tf_op jit(solution)/shard_map/all_to_all | solution.py:64
  141.1 2.9 copy-start.2
  177.5 1.4 copy-start.1
  178.8 5.5 %collective-permute-start = (bf16[1,64,2048]{2,1,0:T(8,128)(2,1)}, bf16[1,64,2048]{2,1,0:T(8,128)(2,1)}, u32[]{:S(2)}, u32[]{:S(2)}) collective-permute-start(bf16[1,64,2048]{2,1,0:T(8,128)(2,1)} %get-tuple-element.74), channel_id=1, source_target_pairs={{0,1},{1,0},{2,3},{3,2},{4,5},{5,4},{6,7},{7,6},{8,9},{9,8},{10,11... | collective-permute-start | bytes 786440 | tf_op jit(solution)/shard_map/ppermute | solution.py:27
  179.0 9.8 %collective-permute-start.1 = (bf16[1,64,2048]{2,1,0:T(8,128)(2,1)}, bf16[1,64,2048]{2,1,0:T(8,128)(2,1)S(1)}, u32[]{:S(2)}, u32[]{:S(2)}) collective-permute-start(bf16[1,64,2048]{2,1,0:T(8,128)(2,1)} %get-tuple-element.73), channel_id=1, source_target_pairs={{0,2},{1,3},{2,0},{3,1},{4,6},{5,7},{6,4},{7,5},{8,10},{9,11},{10,... | collective-permute-start | bytes 786440 | tf_op jit(solution)/shard_map/ppermute | solution.py:27
  179.1 14.5 %collective-permute-start.2 = (bf16[1,64,2048]{2,1,0:T(8,128)(2,1)}, bf16[1,64,2048]{2,1,0:T(8,128)(2,1)S(1)}, u32[]{:S(2)}, u32[]{:S(2)}) collective-permute-start(bf16[1,64,2048]{2,1,0:T(8,128)(2,1)} %get-tuple-element.72), channel_id=1, source_target_pairs={{0,3},{1,2},{2,1},{3,0},{4,7},{5,6},{6,5},{7,4},{8,11},{9,10},{10,... | collective-permute-start | bytes 786440 | tf_op jit(solution)/shard_map/ppermute | solution.py:27
  181.1 33.3 %collective-permute-start.3 = (bf16[1,64,2048]{2,1,0:T(8,128)(2,1)S(1)}, bf16[1,64,2048]{2,1,0:T(8,128)(2,1)S(1)}, u32[]{:S(2)}, u32[]{:S(2)}) collective-permute-start(bf16[1,64,2048]{2,1,0:T(8,128)(2,1)S(1)} %get-tuple-element.71), channel_id=1, source_target_pairs={{0,4},{1,5},{2,6},{3,7},{4,0},{5,1},{6,2},{7,3},{8,12},{9,13},{10,... | collective-permute-start | bytes 786440 | tf_op jit(solution)/shard_map/ppermute | solution.py:27
  183.9 31.2 %collective-permute-start.4 = (bf16[1,64,2048]{2,1,0:T(8,128)(2,1)S(1)}, bf16[1,64,2048]{2,1,0:T(8,128)(2,1)S(1)}, u32[]{:S(2)}, u32[]{:S(2)}) collective-permute-start(bf16[1,64,2048]{2,1,0:T(8,128)(2,1)S(1)} %get-tuple-element.70), channel_id=1, source_target_pairs={{0,5},{1,4},{2,7},{3,6},{4,1},{5,0},{6,3},{7,2},{8,13},{9,12},{10,... | collective-permute-start | bytes 786440 | tf_op jit(solution)/shard_map/ppermute | solution.py:27
  184.3 34.1 %collective-permute-start.5 = (bf16[1,64,2048]{2,1,0:T(8,128)(2,1)S(1)}, bf16[1,64,2048]{2,1,0:T(8,128)(2,1)S(1)}, u32[]{:S(2)}, u32[]{:S(2)}) collective-permute-start(bf16[1,64,2048]{2,1,0:T(8,128)(2,1)S(1)} %get-tuple-element.69), channel_id=1, source_target_pairs={{0,6},{1,7},{2,4},{3,5},{4,2},{5,3},{6,0},{7,1},{8,14},{9,15},{10,... | collective-permute-start | bytes 786440 | tf_op jit(solution)/shard_map/ppermute | solution.py:27
  188.8 34.6 %collective-permute-start.6 = (bf16[1,64,2048]{2,1,0:T(8,128)(2,1)S(1)}, bf16[1,64,2048]{2,1,0:T(8,128)(2,1)S(1)}, u32[]{:S(2)}, u32[]{:S(2)}) collective-permute-start(bf16[1,64,2048]{2,1,0:T(8,128)(2,1)S(1)} %get-tuple-element.68), channel_id=1, source_target_pairs={{0,7},{1,6},{2,5},{3,4},{4,3},{5,2},{6,1},{7,0},{8,15},{9,14},{10,... | collective-permute-start | bytes 786440 | tf_op jit(solution)/shard_map/ppermute | solution.py:27
  193.6 50.7 %collective-permute-start.7 = (bf16[1,64,2048]{2,1,0:T(8,128)(2,1)S(1)}, bf16[1,64,2048]{2,1,0:T(8,128)(2,1)S(1)}, u32[]{:S(2)}, u32[]{:S(2)}) collective-permute-start(bf16[1,64,2048]{2,1,0:T(8,128)(2,1)S(1)} %get-tuple-element.67), channel_id=1, source_target_pairs={{0,8},{1,9},{2,10},{3,11},{4,12},{5,13},{6,14},{7,15},{8,0},{9,1},... | collective-permute-start | bytes 786440 | tf_op jit(solution)/shard_map/ppermute | solution.py:27
  214.4 41.0 %collective-permute-start.8 = (bf16[1,64,2048]{2,1,0:T(8,128)(2,1)S(1)}, bf16[1,64,2048]{2,1,0:T(8,128)(2,1)S(1)}, u32[]{:S(2)}, u32[]{:S(2)}) collective-permute-start(bf16[1,64,2048]{2,1,0:T(8,128)(2,1)S(1)} %get-tuple-element.66), channel_id=1, source_target_pairs={{0,9},{1,8},{2,11},{3,10},{4,13},{5,12},{6,15},{7,14},{8,1},{9,0},... | collective-permute-start | bytes 786440 | tf_op jit(solution)/shard_map/ppermute | solution.py:27
  215.1 46.0 %collective-permute-start.9 = (bf16[1,64,2048]{2,1,0:T(8,128)(2,1)S(1)}, bf16[1,64,2048]{2,1,0:T(8,128)(2,1)S(1)}, u32[]{:S(2)}, u32[]{:S(2)}) collective-permute-start(bf16[1,64,2048]{2,1,0:T(8,128)(2,1)S(1)} %get-tuple-element.65), channel_id=1, source_target_pairs={{0,10},{1,11},{2,8},{3,9},{4,14},{5,15},{6,12},{7,13},{8,2},{9,3},... | collective-permute-start | bytes 786440 | tf_op jit(solution)/shard_map/ppermute | solution.py:27
  218.3 59.7 %collective-permute-start.10 = (bf16[1,64,2048]{2,1,0:T(8,128)(2,1)S(1)}, bf16[1,64,2048]{2,1,0:T(8,128)(2,1)S(1)}, u32[]{:S(2)}, u32[]{:S(2)}) collective-permute-start(bf16[1,64,2048]{2,1,0:T(8,128)(2,1)S(1)} %get-tuple-element.64), channel_id=1, source_target_pairs={{0,11},{1,10},{2,9},{3,8},{4,15},{5,14},{6,13},{7,12},{8,3},{9,2},... | collective-permute-start | bytes 786440 | tf_op jit(solution)/shard_map/ppermute | solution.py:27
  223.4 60.2 %collective-permute-start.11 = (bf16[1,64,2048]{2,1,0:T(8,128)(2,1)S(1)}, bf16[1,64,2048]{2,1,0:T(8,128)(2,1)S(1)}, u32[]{:S(2)}, u32[]{:S(2)}) collective-permute-start(bf16[1,64,2048]{2,1,0:T(8,128)(2,1)S(1)} %get-tuple-element.63), channel_id=1, source_target_pairs={{0,12},{1,13},{2,14},{3,15},{4,8},{5,9},{6,10},{7,11},{8,4},{9,5},... | collective-permute-start | bytes 786440 | tf_op jit(solution)/shard_map/ppermute | solution.py:27
  244.3 44.9 %collective-permute-start.12 = (bf16[1,64,2048]{2,1,0:T(8,128)(2,1)S(1)}, bf16[1,64,2048]{2,1,0:T(8,128)(2,1)S(1)}, u32[]{:S(2)}, u32[]{:S(2)}) collective-permute-start(bf16[1,64,2048]{2,1,0:T(8,128)(2,1)S(1)} %get-tuple-element.62), channel_id=1, source_target_pairs={{0,13},{1,12},{2,15},{3,14},{4,9},{5,8},{6,11},{7,10},{8,5},{9,4},... | collective-permute-start | bytes 786440 | tf_op jit(solution)/shard_map/ppermute | solution.py:27
  255.4 40.5 %collective-permute-start.13 = (bf16[1,64,2048]{2,1,0:T(8,128)(2,1)S(1)}, bf16[1,64,2048]{2,1,0:T(8,128)(2,1)S(1)}, u32[]{:S(2)}, u32[]{:S(2)}) collective-permute-start(bf16[1,64,2048]{2,1,0:T(8,128)(2,1)S(1)} %get-tuple-element.61), channel_id=1, source_target_pairs={{0,14},{1,15},{2,12},{3,13},{4,10},{5,11},{6,8},{7,9},{8,6},{9,7},... | collective-permute-start | bytes 786440 | tf_op jit(solution)/shard_map/ppermute | solution.py:27
  261.2 39.4 %collective-permute-start.14 = (bf16[1,64,2048]{2,1,0:T(8,128)(2,1)S(1)}, bf16[1,64,2048]{2,1,0:T(8,128)(2,1)S(1)}, u32[]{:S(2)}, u32[]{:S(2)}) collective-permute-start(bf16[1,64,2048]{2,1,0:T(8,128)(2,1)S(1)} %get-tuple-element.60), channel_id=1, source_target_pairs={{0,15},{1,14},{2,13},{3,12},{4,11},{5,10},{6,9},{7,8},{8,7},{9,6},... | collective-permute-start | bytes 786440 | tf_op jit(solution)/shard_map/ppermute | solution.py:27
